TPU v7x, 1024 devices: a whole 8x8x8 slice. The times are simulated.
1024 devices in a mesh: lam: 64 (over z, y_hi, core), nu: 16 (over y_lo, x).
Axes of the slice: x: 8, y: 8 (y_hi: 4, y_lo: 2; y = y_hi * 2 + y_lo), z: 8, core: 2. Of those that a mesh axis runs over, the one named last changes fastest.
Arguments:
- integrals: bfloat16 [128, 2048, 2048], P('lam', None, 'nu'), may hold values from -6 to 6
- orbitals: bfloat16 [2048, 512], replicated, may hold values from -0.125 to 0.125
- lam_orbitals: bfloat16 [128, 4], P('lam'), may hold values from -0.5 to 0.5
Outputs:
- transformed: float32 [4, 512, 512], P(None, 'nu', 'lam')
All inputs are finite; a program needn't handle non-finite values.
Results may differ from a plain program's by a relative error of at most 0.0029.
Values may be sent and summed in bfloat16 or wider, within the bound.
No kernel may reach another device: no remote copies, remote signals or barrier semaphores. Data moves between devices by JAX's collectives and lax.ppermute only.
A program may use at most 32 MiB of HBM per device.

v0:
```python
import jax
import jax.numpy as jnp
from jax import lax
from jax.sharding import PartitionSpec as P


def shards(integrals, orbitals, lam_orbitals):
    halfway = jnp.einsum(
        "lmn,mi->lin", integrals, orbitals, preferred_element_type=jnp.float32
    ).astype(jnp.bfloat16)
    exchanged = lax.all_to_all(halfway, "nu", split_axis=1, concat_axis=2, tiled=True)
    second = jnp.einsum("lin,nj->lij", exchanged, orbitals, preferred_element_type=jnp.float32)
    lam_weights = lam_orbitals.astype(jnp.float32)
    partial_terms = jnp.einsum("lij,lk->jki", second, lam_weights, precision=lax.Precision.HIGHEST)
    summed = lax.psum_scatter(partial_terms, "lam", scatter_dimension=0, tiled=True)
    return jnp.transpose(summed, (1, 2, 0))


def solution(mesh):
    return jax.shard_map(
        shards,
        mesh=mesh,
        in_specs=(P("lam", None, "nu"), P(), P("lam", None)),
        out_specs=P(None, "nu", "lam"),
        check_vma=False,
    )
```

profile of v0, /device:TPU:1, one launch (start us, length us, event | category | flops | bytes accessed | tf_op | source)
XLA Modules:
  0.0 612.7 jit_solution(14498820099943805948)
XLA Ops:
  6.5 0.0 copy-start
  6.5 0.0 all-reduce.3.cloned.1.call-start
  6.5 1.6 copy-done
  8.1 2.0 fusion.7
  10.1 0.3 copy.10
  10.4 0.0 copy-start.1
  10.4 16.1 %all_to_all.18 = bf16[2,512,128]{2,0,1:T(2,128)(2,1)S(1)} all-to-all(bf16[2,512,128]{2,0,1:T(2,128)(2,1)S(1)} %copy.10), channel_id=1, replica_groups=mesh['lam'=64,'nu'=16] {'nu'}, dimensions={1} | all-to-all | bytes 524288 | tf_op jit(solution)/shard_map/all_to_all | solution.py:11
  26.5 0.2 copy.20
  26.7 0.1 all_to_all.16
  26.8 0.5 fusion
  27.3 0.0 copy-done.1
  27.3 0.4 convolution_bitcast_fusion
  27.7 1.4 copy.13
  29.1 0.0 all-reduce.3.cloned.1.call-update
  29.1 1.3 dynamic-slice
  31.1 573.4 %all-reduce.3.cloned.1.call-done = f32[512,4,32]{2,1,0:T(4,128)} async-done(((f32[512,4,32]{2,1,0:T(4,128)}), f32[512,4,32]{2,1,0:T(4,128)}) %all-reduce.3.cloned.1.call-update) | async-done | bytes 262160
  604.5 0.7 dynamic-slice_bitcast_fusion
  605.2 0.6 copy.14
Async XLA Ops:
  6.5 1.6 copy-start
  6.5 598.0 %all-reduce.3.cloned.1.call-start = ((), (), s32[]{:S(2)}) async-start(), calls=%async_computation.1 | async-start | bytes 2097152
  10.4 16.9 %copy-start.1 = (bf16[2,4]{1,0:T(2,128)(2,1)S(1)}, bf16[2,4]{1,0:T(2,128)(2,1)}, u32[]{:S(2)}) copy-start(bf16[2,4]{1,0:T(2,128)(2,1)} %param.5) | copy-start | bytes 52
Sparse Core Ops, SparseCore 0:
  29.2 575.2 all-reduce.2
where the time goes:
time: 613 us
  waiting for transfers between devices  573 us (93%)
  blocking collectives  16.1 us (3%)
  between operations  14.1 us (2%)
  local copies, waits for them, and re-layouts  6.14 us (1%)
    unnamed x2, waiting for transfers between devices  573 us
    all_to_all x1, blocking collectives, shards(): lax.all_to_all(halfway, 'nu', split_axis=1, concat_axis=2, tiled=True)  16.1 us
  transfers between devices with their start and end apart: 1, of which 1 were waited for; matrix products, arithmetic and copies ran while one was open for 0% of the time, Pallas kernels for 0%

commit v1 on v0

v1 whole, which is shorter than its diff:
```python
import jax
import jax.numpy as jnp
from jax import lax
from jax.sharding import PartitionSpec as P


def shards(integrals, orbitals, lam_orbitals):
    halfway = jnp.einsum(
        "lmn,mi->lin", integrals, orbitals, preferred_element_type=jnp.float32
    ).astype(jnp.bfloat16)
    halfway = halfway.reshape(2, 16, 32, 128).transpose(1, 0, 2, 3)
    exchanged = lax.all_to_all(halfway, "nu", split_axis=0, concat_axis=0, tiled=True)
    weights = lam_orbitals.astype(jnp.float32)
    rows = exchanged.transpose(1, 2, 0, 3).reshape(64, 2048)
    second = jnp.einsum("nj,rn->jr", orbitals, rows, preferred_element_type=jnp.float32)
    s0, s1 = second[:, :32], second[:, 32:]
    terms = jnp.concatenate([s0 * weights[0, k] + s1 * weights[1, k] for k in range(4)], axis=1)
    sent = terms.astype(jnp.bfloat16).reshape(64, 8, 128)
    received = lax.all_to_all(sent, "lam", split_axis=0, concat_axis=0, tiled=True)
    summed = jnp.sum(received.astype(jnp.float32), axis=0)
    return summed.reshape(8, 4, 32).transpose(1, 2, 0)


def solution(mesh):
    return jax.shard_map(
        shards,
        mesh=mesh,
        in_specs=(P("lam", None, "nu"), P(), P("lam", None)),
        out_specs=P(None, "nu", "lam"),
        check_vma=False,
    )
```

time: 613 us -> 66.9 us (0.11)
  waiting for transfers between devices: 573 us -> 7.07 us
  blocking collectives: 16.1 us -> 38.7 us
  between operations: 14.1 us -> 0.08 us
  starting transfers between devices: 0.01 us -> 8.54 us
    unnamed x2 -> x0, waiting for transfers between devices: 573 us -> none
    all_to_all x1, blocking collectives: 16.1 us -> 38.7 us  [shards(): lax.all_to_all(sent, 'lam', split_axis=0, concat_axis=0, tiled=True)]
    all_to_all x0 -> x1, starting transfers between devices: none -> 8.54 us  [shards(): lax.all_to_all(halfway, 'nu', split_axis=0, concat_axis=0, tiled=True)]
    all_to_all x0 -> x1, waiting for transfers between devices: none -> 7.07 us  [shards(): lax.all_to_all(halfway, 'nu', split_axis=0, concat_axis=0, tiled=True)]
  transfers between devices with their start and end apart: 1 -> 1, of which waited for: 1 -> 1; matrix products, arithmetic and copies ran while one was open for 0% -> 1% of each run, Pallas kernels for 0% -> 0%
where the time goes in v1:
time: 66.9 us; the launch traced here: 66.5 us
  blocking collectives  38.7 us (58%)
  starting transfers between devices  8.54 us (13%)
  waiting for transfers between devices  7.07 us (11%)
  other arithmetic  5.37 us (8%)
  local copies, waits for them, and re-layouts  4.35 us (7%)
  matrix products  2.44 us (4%)
    all_to_all x1, blocking collectives, shards(): lax.all_to_all(sent, 'lam', split_axis=0, concat_axis=0, tiled=True)  38.7 us
    all_to_all x1, starting transfers between devices, shards(): lax.all_to_all(halfway, 'nu', split_axis=0, concat_axis=0, tiled=True)  8.54 us
    all_to_all x1, waiting for transfers between devices, shards(): lax.all_to_all(halfway, 'nu', split_axis=0, concat_axis=0, tiled=True)  7.07 us
    another operation x1, other arithmetic  5.11 us
    dot_general x1, matrix products, shards(): jnp.einsum('lmn,mi->lin', integrals, orbitals, preferred_element_type=jnp...  1.99 us
    unnamed x4, local copies, waits for them, and re-layouts  1.59 us
  transfers between devices with their start and end apart: 1, of which 1 were waited for; matrix products, arithmetic and copies ran while one was open for 1% of the time, Pallas kernels for 0%

profile of v1, /device:TPU:1, one launch (start us, length us, event | category | flops | bytes accessed | tf_op | source)
XLA Modules:
  0.0 66.5 jit_solution(7179854266683171265)
XLA Ops:
  0.0 0.0 copy-start
  0.0 1.6 %copy-done = bf16[2048,512]{1,0:T(8,128)(2,1)S(1)} copy-done((bf16[2048,512]{1,0:T(8,128)(2,1)S(1)}, bf16[2048,512]{1,0:T(8,128)(2,1)}, u32[]{:S(2)}) %copy-start) | copy-done | bytes 2097176
  1.6 0.0 copy-start.1
  1.6 2.0 %fusion.2 = bf16[512,2,128]{2,0,1:T(8,128)(2,1)S(1)} fusion(bf16[2,2048,128]{2,1,0:T(8,128)(2,1)} %param.3, bf16[2048,512]{1,0:T(8,128)(2,1)S(1)} %copy-done), kind=kOutput, calls=%fused_computation.2 | convolution fusion | flops 537001984 | bytes 3407872 | tf_op jit(solution)/shard_map/lmn,mi->lin/dot_general | solution.py:8
  3.6 0.7 %copy.28 = bf16[2,16,32,128]{3,2,0,1:T(8,128)(2,1)} copy(bf16[2,16,32,128]{3,2,1,0:T(8,128)(2,1)S(1)} %bitcast.40) | data formatting | bytes 524288 | tf_op jit(solution)/shard_map/reshape | solution.py:11
  4.3 8.5 %all-to-all-start = ((bf16[16,2,32,128]{3,2,1,0:T(8,128)(2,1)}), bf16[16,2,32,128]{3,2,1,0:T(8,128)(2,1)S(1)}, u32[]{:S(2)}, u32[]{:S(2)}) async-start(bf16[16,2,32,128]{3,2,1,0:T(8,128)(2,1)} %bitcast.33), calls=%async_computation | async-start | bytes 524288 | tf_op jit(solution)/shard_map/all_to_all | solution.py:12
  12.9 0.0 copy-done.1
  12.9 0.7 %fusion.7 = (f32[1,1]{1,0:T(1,128)}, f32[1,1]{1,0:T(1,128)}, f32[1,1]{1,0:T(1,128)}, f32[1,1]{1,0:T(1,128)}, f32[1,1]{1,0:T(1,128)}, /*index=5*/f32[1,1]{1,0:T(1,128)}, f32[1,1]{1,0:T(1,128)}, f32[1,1]{1,0:T(1,128)}) fusion(bf16[2,4]{1,0:T(2,128)(2,1)S(1)} %copy-done.1), kind=kLoop, calls=%fused_computation.13 | loop fusion | bytes 64 | tf_op jit(solution)/shard_map/slice | solution.py:17
  13.5 7.1 %all-to-all-done = bf16[16,2,32,128]{3,2,1,0:T(8,128)(2,1)S(1)} async-done(((bf16[16,2,32,128]{3,2,1,0:T(8,128)(2,1)}), bf16[16,2,32,128]{3,2,1,0:T(8,128)(2,1)S(1)}, u32[]{:S(2)}, u32[]{:S(2)}) %all-to-all-start) | async-done | bytes 262176 | tf_op jit(solution)/shard_map/all_to_all | solution.py:12
  20.6 0.2 copy.14
  20.8 0.4 convolution_bitcast_fusion
  21.3 5.1 %add_convert_fusion.3 = (bf16[512,32]{0,1:T(8,128)(2,1)S(1)}, bf16[512,32]{0,1:T(8,128)(2,1)S(1)}, bf16[512,32]{0,1:T(8,128)(2,1)S(1)}, bf16[512,32]{0,1:T(8,128)(2,1)S(1)}) fusion(f32[512,64]{0,1:T(8,128)S(1)} %convolution_bitcast_fusion, f32[]{:T(128)} %bitcast.7, f32[]{:T(128)} %bitcast.6, f32[]{:T(128)} %bitcast.13, f32[]{:T(128)} %bitcast.12, ...), kind=kLoop, calls=%fused_computation.12 | loop fusion | flops 262144 | bytes 262176 | tf_op jit(solution)/shard_map/convert.7
  26.4 0.1 copy.15
  26.5 0.1 copy.17
  26.6 0.1 copy.18
  26.8 0.1 copy.16
  26.9 0.2 pad_maximum_fusion
  27.1 38.7 %all_to_all.10 = bf16[64,8,128]{2,1,0:T(8,128)(2,1)S(1)} all-to-all(bf16[64,8,128]{2,1,0:T(8,128)(2,1)S(1)} %pad_maximum_fusion), channel_id=1, replica_groups=mesh['lam'=64,'nu'=16] {'lam'}, dimensions={0} | all-to-all | bytes 262144 | tf_op jit(solution)/shard_map/all_to_all | solution.py:19
  65.8 0.1 convert_reduce_fusion
  65.8 0.1 reshape.20
  65.9 0.6 copy.19
Async XLA Ops:
  0.0 1.6 %copy-start = (bf16[2048,512]{1,0:T(8,128)(2,1)S(1)}, bf16[2048,512]{1,0:T(8,128)(2,1)}, u32[]{:S(2)}) copy-start(bf16[2048,512]{1,0:T(8,128)(2,1)} %param.4) | copy-start | bytes 6291460
  1.6 11.3 %copy-start.1 = (bf16[2,4]{1,0:T(2,128)(2,1)S(1)}, bf16[2,4]{1,0:T(2,128)(2,1)}, u32[]{:S(2)}) copy-start(bf16[2,4]{1,0:T(2,128)(2,1)} %param.5) | copy-start | bytes 52
  4.3 16.3 %all-to-all-start = ((bf16[16,2,32,128]{3,2,1,0:T(8,128)(2,1)}), bf16[16,2,32,128]{3,2,1,0:T(8,128)(2,1)S(1)}, u32[]{:S(2)}, u32[]{:S(2)}) async-start(bf16[16,2,32,128]{3,2,1,0:T(8,128)(2,1)} %bitcast.33), calls=%async_computation | async-start | bytes 524288 | tf_op jit(solution)/shard_map/all_to_all | solution.py:12

commit v2 on v0

v2 whole, which is shorter than its diff:
```python
import functools

import jax
import jax.numpy as jnp
from jax import lax
from jax.experimental import pallas as pl
from jax.experimental.pallas import tpu as pltpu
from jax.sharding import PartitionSpec as P

CHUNKS = 4
VMEM_LIMIT = 16 << 20
NU_FIRST = 12
LAM_FIRST = 36


def turned(size, start):
    return [(start + p) % size for p in range(size)]


def first_kernel(integrals_hbm, orbitals_hbm, out_ref, orbitals, integrals, sems):
    lams, mus, _ = integrals.shape
    owners = out_ref.shape[0]
    size = mus // CHUNKS
    copies = []
    for c in range(CHUNKS):
        rows = pl.ds(c * size, size)
        copies.append(
            (
                pltpu.make_async_copy(orbitals_hbm.at[rows], orbitals.at[rows], sems.at[0, c]),
                pltpu.make_async_copy(integrals_hbm.at[:, rows], integrals.at[:, rows], sems.at[1, c]),
            )
        )
    for pair in copies:
        for copy in pair:
            copy.start()
    totals = [None] * lams
    for c in range(CHUNKS):
        for copy in copies[c]:
            copy.wait()
        rows = pl.ds(c * size, size)
        block = orbitals[rows, :]
        for l in range(lams):
            term = lax.dot_general(
                block, integrals[l, rows, :], (((0,), (0,)), ((), ())), preferred_element_type=jnp.float32
            )
            totals[l] = term if c == 0 else totals[l] + term
    for l in range(lams):
        total = totals[l].astype(out_ref.dtype)
        width = total.shape[0] // owners
        for p, owner in enumerate(turned(owners, NU_FIRST)):
            out_ref[p, l * width : (l + 1) * width, :] = total[owner * width : (owner + 1) * width]


def first(integrals, orbitals, owners):
    lams, mus, ns = integrals.shape
    orbs = orbitals.shape[1]
    return pl.pallas_call(
        first_kernel,
        out_shape=(
            pltpu.VMEM((owners, lams * orbs // owners, ns), integrals.dtype),
            pltpu.VMEM(orbitals.shape, orbitals.dtype),
        ),
        in_specs=[pl.BlockSpec(memory_space=pltpu.HBM), pl.BlockSpec(memory_space=pltpu.HBM)],
        out_specs=(pl.BlockSpec(memory_space=pltpu.VMEM), pl.BlockSpec(memory_space=pltpu.VMEM)),
        scratch_shapes=[
            pltpu.VMEM(integrals.shape, integrals.dtype),
            pltpu.SemaphoreType.DMA((2, CHUNKS)),
        ],
        compiler_params=pltpu.CompilerParams(vmem_limit_bytes=VMEM_LIMIT),
    )(*(pltpu.with_memory_space_constraint(x, pltpu.HBM) for x in (integrals, orbitals)))


def second_kernel(weights_ref, rows_ref, orbitals_ref, out_ref):
    lams, korb = weights_ref.shape
    owners, height, ns = rows_ref.shape
    step = 2
    total = None
    for s in range(0, owners, step):
        left = jnp.concatenate([rows_ref[s + t] for t in range(step)], axis=1)
        owner = (s + NU_FIRST) % owners
        right = orbitals_ref[owner * ns : (owner + step) * ns, :]
        term = jnp.dot(left, right, preferred_element_type=jnp.float32)
        total = term if total is None else total + term
    width = height // lams
    weights = weights_ref[...].astype(jnp.float32)
    terms = []
    for k in range(korb):
        term = weights[0:1, k : k + 1] * total[:width]
        for l in range(1, lams):
            term = term + weights[l : l + 1, k : k + 1] * total[l * width : (l + 1) * width]
        terms.append(term)
    sent = jnp.concatenate(terms, axis=0).T
    sent = sent.reshape(out_ref.shape).astype(out_ref.dtype)
    out_ref[: out_ref.shape[0] - LAM_FIRST] = sent[LAM_FIRST:]
    out_ref[out_ref.shape[0] - LAM_FIRST :] = sent[:LAM_FIRST]


def second(weights, rows, orbitals, owners):
    _, height, _ = rows.shape
    lams, korb = weights.shape
    orbs = orbitals.shape[1]
    vmem = pl.BlockSpec(memory_space=pltpu.VMEM)
    return pl.pallas_call(
        second_kernel,
        out_shape=pltpu.VMEM((owners, orbs // owners, korb * height // lams), rows.dtype),
        in_specs=[vmem, vmem, vmem],
        out_specs=vmem,
        compiler_params=pltpu.CompilerParams(vmem_limit_bytes=VMEM_LIMIT),
    )(*(pltpu.with_memory_space_constraint(x, pltpu.VMEM) for x in (weights, rows, orbitals)))


def shards(lam_owners, nu_owners, integrals, orbitals, lam_orbitals):
    halfway, orbitals = first(integrals, orbitals, nu_owners)
    exchanged = lax.all_to_all(
        halfway, "nu", split_axis=0, concat_axis=0, tiled=True, axis_index_groups=[turned(nu_owners, NU_FIRST)]
    )
    sent = second(lam_orbitals, exchanged, orbitals, lam_owners)
    received = lax.all_to_all(
        sent, "lam", split_axis=0, concat_axis=0, tiled=True, axis_index_groups=[turned(lam_owners, LAM_FIRST)]
    )
    summed = jnp.sum(received.astype(jnp.float32), axis=0)
    korb = lam_orbitals.shape[1]
    return summed.reshape(summed.shape[0], korb, -1).transpose(1, 2, 0)


def solution(mesh):
    return jax.shard_map(
        functools.partial(shards, mesh.shape["lam"], mesh.shape["nu"]),
        mesh=mesh,
        in_specs=(P("lam", None, "nu"), P(), P("lam", None)),
        out_specs=P(None, "nu", "lam"),
        check_vma=False,
    )
```

time: 613 us -> 51.8 us (0.08)
  waiting for transfers between devices: 573 us -> 0 us
  blocking collectives: 16.1 us -> 47.4 us
  between operations: 14.1 us -> 0.02 us
    unnamed x2 -> x0, waiting for transfers between devices: 573 us -> none
    all_to_all x1 -> x2, blocking collectives: 16.1 us -> 47.4 us  [the longest x1 33.5 us: shards(): lax.all_to_all(sent, 'lam', split_axis=0, concat_axis=0, tiled=True, axis...]
  transfers between devices with their start and end apart: 1 -> 0, of which waited for: 1 -> 0; matrix products, arithmetic and copies ran while one was open for 0% -> 0% of each run, Pallas kernels for 0% -> 0%
where the time goes in v2:
time: 51.8 us; the launch traced here: 51.6 us
  blocking collectives  47.4 us (92%)
  Pallas kernels  3.47 us (7%)
  local copies, waits for them, and re-layouts  0.7 us (1%)
    all_to_all x1, blocking collectives, shards(): lax.all_to_all(sent, 'lam', split_axis=0, concat_axis=0, tiled=True, axis...  33.5 us
    all_to_all x1, blocking collectives, shards(): lax.all_to_all(halfway, 'nu', split_axis=0, concat_axis=0, tiled=True, ax...  13.8 us
    pallas_call x1, Pallas kernels, first(): pl.pallas_call(first_kernel, out_shape=(pltpu.VMEM((owners, lams * orbs /...  2.88 us

profile of v2, /device:TPU:1, one launch (start us, length us, event | category | flops | bytes accessed | tf_op | source)
XLA Modules:
  0.0 51.6 jit_solution(1029713255881579073)
XLA Ops:
  0.0 0.0 copy-start
  0.0 2.9 %shard_map.37 = (bf16[16,64,128]{2,1,0:T(8,128)(2,1)S(1)}, bf16[2048,512]{1,0:T(8,128)(2,1)S(1)}) custom-call(bf16[2,2048,128]{2,1,0:T(8,128)(2,1)} %integrals_hbm.1, bf16[2048,512]{1,0:T(8,128)(2,1)} %orbitals_hbm.1), custom_call_target="tpu_custom_call" | custom-call | tf_op jit(solution)/shard_map/pallas_call | solution.py:57
  2.9 13.8 %all_to_all.10.rows_ref = bf16[16,64,128]{2,1,0:T(8,128)(2,1)S(1)} all-to-all(bf16[16,64,128]{2,1,0:T(8,128)(2,1)S(1)} %get-tuple-element.7), channel_id=1, replica_groups={{12,13,14,15,0,1,2,3,4,5,6,7,8,9,10,11},{28,29,30,31,16,17,18,19,20,21,..., dimensions={0} | all-to-all | bytes 524288 | tf_op jit(solution)/shard_map/all_to_all | solution.py:114
  16.7 0.0 copy-done
  16.7 0.6 %shard_map.38 = bf16[64,8,128]{2,1,0:T(8,128)(2,1)S(1)} custom-call(bf16[2,4]{1,0:T(2,128)(2,1)S(1)} %copy-done, bf16[16,64,128]{2,1,0:T(8,128)(2,1)S(1)} %all_to_all.10.rows_ref, bf16[2048,512]{1,0:T(8,128)(2,1)S(1)} %get-tuple-element.8.orbitals_ref), custom_call_target="tpu_custom_call" | custom-call | tf_op jit(solution)/shard_map/pallas_call | solution.py:103
  17.3 33.5 %all_to_all.11 = bf16[64,8,128]{2,1,0:T(8,128)(2,1)S(1)} all-to-all(bf16[64,8,128]{2,1,0:T(8,128)(2,1)S(1)} %shard_map.38), channel_id=1, replica_groups={{576,592,608,624,640,656,672,688,704,720,736,752,768,784,800,816,832,84..., dimensions={0} | all-to-all | bytes 262144 | tf_op jit(solution)/shard_map/all_to_all | solution.py:118
  50.9 0.1 convert_reduce_fusion
  51.0 0.1 reshape.3
  51.0 0.6 %copy.4 = f32[4,32,8]{1,2,0:T(8,128)} copy(f32[4,32,8]{1,0,2:T(4,128)S(1)} %bitcast.1) | data formatting | bytes 8192 | tf_op jit(solution)/shard_map/transpose | solution.py:123
Async XLA Ops:
  0.0 16.7 %copy-start = (bf16[2,4]{1,0:T(2,128)(2,1)S(1)}, bf16[2,4]{1,0:T(2,128)(2,1)}, u32[]{:S(2)}) copy-start(bf16[2,4]{1,0:T(2,128)(2,1)} %weights_ref.1) | copy-start | bytes 52

commit v3 on v2

v3 whole, which is shorter than its diff:
```python
import functools

import jax
import jax.numpy as jnp
from jax import lax
from jax.experimental import pallas as pl
from jax.experimental.pallas import tpu as pltpu
from jax.sharding import PartitionSpec as P

CHUNKS = 4
VMEM_LIMIT = 16 << 20
VMEM = pl.BlockSpec(memory_space=pltpu.VMEM)
HBM = pl.BlockSpec(memory_space=pltpu.HBM)
PARAMS = pltpu.CompilerParams(vmem_limit_bytes=VMEM_LIMIT)


def nu_order(size):
    return [(12 + p) % size for p in range(size)]


def lam_order(size):
    return [(45 + p) % size for p in range(size)]


def first_kernel(integrals_hbm, orbitals_hbm, out_ref, orbitals, integrals, sems):
    lams, mus, ns = integrals.shape
    owners = out_ref.shape[0]
    size = mus // CHUNKS
    copies = []
    for c in range(CHUNKS):
        rows = pl.ds(c * size, size)
        copies.append(
            (
                pltpu.make_async_copy(orbitals_hbm.at[rows], orbitals.at[rows], sems.at[0, c]),
                pltpu.make_async_copy(integrals_hbm.at[:, rows], integrals.at[:, rows], sems.at[1, c]),
            )
        )
    for pair in copies:
        for copy in pair:
            copy.start()
    total = None
    for c in range(CHUNKS):
        for copy in copies[c]:
            copy.wait()
        rows = pl.ds(c * size, size)
        block = jnp.concatenate([integrals[l, rows, :].T for l in range(lams)], axis=0)
        term = jnp.dot(block, orbitals[rows, :], preferred_element_type=jnp.float32)
        total = term if total is None else total + term
    total = total.astype(out_ref.dtype)
    width = total.shape[1] // owners
    for l in range(lams):
        block = total[l * ns : (l + 1) * ns].T
        for p, owner in enumerate(nu_order(owners)):
            out_ref[p, l * width : (l + 1) * width, :] = block[owner * width : (owner + 1) * width]


def first(integrals, orbitals, owners):
    lams, _, ns = integrals.shape
    orbs = orbitals.shape[1]
    return pl.pallas_call(
        first_kernel,
        out_shape=(
            pltpu.VMEM((owners, lams * orbs // owners, ns), integrals.dtype),
            pltpu.VMEM(orbitals.shape, orbitals.dtype),
        ),
        in_specs=[HBM, HBM],
        out_specs=(VMEM, VMEM),
        scratch_shapes=[
            pltpu.VMEM(integrals.shape, integrals.dtype),
            pltpu.SemaphoreType.DMA((2, CHUNKS)),
        ],
        compiler_params=PARAMS,
    )(*(pltpu.with_memory_space_constraint(x, pltpu.HBM) for x in (integrals, orbitals)))


def second_kernel(weights_ref, rows_ref, orbitals_ref, out_ref):
    lams, korb = weights_ref.shape
    owners, height, ns = rows_ref.shape
    place = {owner: p for p, owner in enumerate(nu_order(owners))}
    step = 2
    total = None
    for s in range(0, owners, step):
        left = jnp.concatenate([rows_ref[place[s + t]] for t in range(step)], axis=1)
        right = orbitals_ref[s * ns : (s + step) * ns, :]
        term = jnp.dot(left, right, preferred_element_type=jnp.float32)
        total = term if total is None else total + term
    width = height // lams
    weights = weights_ref[...].astype(jnp.float32)
    terms = []
    for k in range(korb):
        term = weights[0:1, k : k + 1] * total[:width]
        for l in range(1, lams):
            term = term + weights[l : l + 1, k : k + 1] * total[l * width : (l + 1) * width]
        terms.append(term)
    sent = jnp.concatenate(terms, axis=0).T
    sent = sent.reshape(out_ref.shape).astype(out_ref.dtype)
    for p, owner in enumerate(lam_order(out_ref.shape[0])):
        out_ref[p] = sent[owner]


def second(weights, rows, orbitals, owners):
    _, height, _ = rows.shape
    lams, korb = weights.shape
    orbs = orbitals.shape[1]
    return pl.pallas_call(
        second_kernel,
        out_shape=pltpu.VMEM((owners, orbs // owners, korb * height // lams), rows.dtype),
        in_specs=[VMEM, VMEM, VMEM],
        out_specs=VMEM,
        compiler_params=PARAMS,
    )(*(pltpu.with_memory_space_constraint(x, pltpu.VMEM) for x in (weights, rows, orbitals)))


def last_kernel(terms_ref, out_ref):
    korb, _, width = out_ref.shape
    total = jnp.sum(terms_ref[...].astype(jnp.float32), axis=0)
    for k in range(korb):
        out_ref[k] = total[:, k * width : (k + 1) * width]


def last(terms, korb):
    _, js, height = terms.shape
    return pl.pallas_call(
        last_kernel,
        out_shape=jax.ShapeDtypeStruct((korb, js, height // korb), jnp.float32),
        in_specs=[VMEM],
        out_specs=VMEM,
        compiler_params=PARAMS,
    )(pltpu.with_memory_space_constraint(terms, pltpu.VMEM))


def exchange(blocks, axis, order):
    return lax.all_to_all(blocks, axis, split_axis=0, concat_axis=0, tiled=True, axis_index_groups=[order])


def shards(lam_owners, nu_owners, integrals, orbitals, lam_orbitals):
    halfway, orbitals = first(integrals, orbitals, nu_owners)
    rows = exchange(halfway, "nu", nu_order(nu_owners))
    sent = second(lam_orbitals, rows, orbitals, lam_owners)
    terms = exchange(sent, "lam", lam_order(lam_owners))
    return last(terms, lam_orbitals.shape[1]).transpose(0, 2, 1)


def solution(mesh):
    return jax.shard_map(
        functools.partial(shards, mesh.shape["lam"], mesh.shape["nu"]),
        mesh=mesh,
        in_specs=(P("lam", None, "nu"), P(), P("lam", None)),
        out_specs=P(None, "nu", "lam"),
        check_vma=False,
    )
```

time: 51.8 us -> 50.5 us (0.975)
  blocking collectives: 47.4 us -> 46.6 us
  local copies, waits for them, and re-layouts: 0.7 us -> 0.01 us
    all_to_all x2, blocking collectives: 47.4 us -> 46.6 us  [exchange(): lax.all_to_all(blocks, axis, split_axis=0, concat_axis=0, tiled=True, axi...]
    pallas_call x0 -> x1, Pallas kernels: none -> 0.74 us  [last(): pl.pallas_call(last_kernel, out_shape=jax.ShapeDtypeStruct((korb, js, hei...]
    transpose x1 -> x0, local copies, waits for them, and re-layouts: 0.61 us -> none  [shards(): return summed.reshape(summed.shape[0], korb, -1).transpose(1, 2, 0)]
where the time goes in v3:
time: 50.5 us; the launch traced here: 50.4 us
  blocking collectives  46.6 us (92%)
  Pallas kernels  3.74 us (7%)
    all_to_all x2, blocking collectives, exchange(): lax.all_to_all(blocks, axis, split_axis=0, concat_axis=0, tiled=True, axi...  46.6 us
    pallas_call x1, Pallas kernels, first(): pl.pallas_call(first_kernel, out_shape=(pltpu.VMEM((owners, lams * orbs /...  2.41 us

profile of v3, /device:TPU:1, one launch (start us, length us, event | category | flops | bytes accessed | tf_op | source)
XLA Modules:
  0.0 50.4 jit_solution(8916869280902832429)
XLA Ops:
  0.0 0.0 copy-start
  0.0 2.4 %shard_map.37 = (bf16[16,64,128]{2,1,0:T(8,128)(2,1)S(1)}, bf16[2048,512]{1,0:T(8,128)(2,1)S(1)}) custom-call(bf16[2,2048,128]{2,1,0:T(8,128)(2,1)} %integrals_hbm.1, bf16[2048,512]{1,0:T(8,128)(2,1)} %orbitals_hbm.1), custom_call_target="tpu_custom_call" | custom-call | tf_op jit(solution)/shard_map/pallas_call | solution.py:60
  2.4 13.8 %all_to_all.10.rows_ref = bf16[16,64,128]{2,1,0:T(8,128)(2,1)S(1)} all-to-all(bf16[16,64,128]{2,1,0:T(8,128)(2,1)S(1)} %get-tuple-element.7), channel_id=1, replica_groups={{12,13,14,15,0,1,2,3,4,5,6,7,8,9,10,11},{28,29,30,31,16,17,18,19,20,21,..., dimensions={0} | all-to-all | bytes 524288 | tf_op jit(solution)/shard_map/all_to_all | solution.py:133
  16.3 0.0 copy-done
  16.3 0.6 %shard_map.38 = bf16[64,8,128]{2,1,0:T(8,128)(2,1)S(1)} custom-call(bf16[2,4]{1,0:T(2,128)(2,1)S(1)} %copy-done, bf16[16,64,128]{2,1,0:T(8,128)(2,1)S(1)} %all_to_all.10.rows_ref, bf16[2048,512]{1,0:T(8,128)(2,1)S(1)} %get-tuple-element.8.orbitals_ref), custom_call_target="tpu_custom_call" | custom-call | tf_op jit(solution)/shard_map/pallas_call | solution.py:105
  16.9 32.7 %all_to_all.11.terms_ref = bf16[64,8,128]{2,1,0:T(8,128)(2,1)S(1)} all-to-all(bf16[64,8,128]{2,1,0:T(8,128)(2,1)S(1)} %shard_map.38), channel_id=1, replica_groups={{720,736,752,768,784,800,816,832,848,864,880,896,912,928,944,960,976,99..., dimensions={0} | all-to-all | bytes 262144 | tf_op jit(solution)/shard_map/all_to_all | solution.py:133
  49.6 0.7 %shard_map.39 = f32[4,8,32]{2,1,0:T(8,128)} custom-call(bf16[64,8,128]{2,1,0:T(8,128)(2,1)S(1)} %all_to_all.11.terms_ref), custom_call_target="tpu_custom_call" | custom-call | tf_op jit(solution)/shard_map/pallas_call | solution.py:123
Async XLA Ops:
  0.0 16.3 %copy-start = (bf16[2,4]{1,0:T(2,128)(2,1)S(1)}, bf16[2,4]{1,0:T(2,128)(2,1)}, u32[]{:S(2)}) copy-start(bf16[2,4]{1,0:T(2,128)(2,1)} %weights_ref.1) | copy-start | bytes 52

commit v4 on v3

--- a/solution.py
+++ b/solution.py
@@ -92,8 +92,8 @@
         for l in range(1, lams):
             term = term + weights[l : l + 1, k : k + 1] * total[l * width : (l + 1) * width]
         terms.append(term)
-    sent = jnp.concatenate(terms, axis=0).T
-    sent = sent.reshape(out_ref.shape).astype(out_ref.dtype)
+    sent = jnp.concatenate(terms, axis=0).astype(out_ref.dtype).T
+    sent = sent.reshape(out_ref.shape)
     for p, owner in enumerate(lam_order(out_ref.shape[0])):
         out_ref[p] = sent[owner]
 

time: 50.5 us -> 50.5 us (level)
  no operation moved by 1% of the time
where the time goes in v4:
time: 50.5 us; the launch traced here: 50.3 us
  blocking collectives  46.6 us (92%)
  Pallas kernels  3.73 us (7%)
    all_to_all x2, blocking collectives, exchange(): lax.all_to_all(blocks, axis, split_axis=0, concat_axis=0, tiled=True, axi...  46.6 us
    pallas_call x1, Pallas kernels, first(): pl.pallas_call(first_kernel, out_shape=(pltpu.VMEM((owners, lams * orbs /...  2.41 us

profile of v4, /device:TPU:1, one launch (start us, length us, event | category | flops | bytes accessed | tf_op | source)
XLA Modules:
  0.0 50.3 jit_solution(7635551375429620022)
XLA Ops:
  0.0 0.0 copy-start
  0.0 2.4 %shard_map.37 = (bf16[16,64,128]{2,1,0:T(8,128)(2,1)S(1)}, bf16[2048,512]{1,0:T(8,128)(2,1)S(1)}) custom-call(bf16[2,2048,128]{2,1,0:T(8,128)(2,1)} %integrals_hbm.1, bf16[2048,512]{1,0:T(8,128)(2,1)} %orbitals_hbm.1), custom_call_target="tpu_custom_call" | custom-call | tf_op jit(solution)/shard_map/pallas_call | solution.py:60
  2.4 13.8 %all_to_all.10.rows_ref = bf16[16,64,128]{2,1,0:T(8,128)(2,1)S(1)} all-to-all(bf16[16,64,128]{2,1,0:T(8,128)(2,1)S(1)} %get-tuple-element.7), channel_id=1, replica_groups={{12,13,14,15,0,1,2,3,4,5,6,7,8,9,10,11},{28,29,30,31,16,17,18,19,20,21,..., dimensions={0} | all-to-all | bytes 524288 | tf_op jit(solution)/shard_map/all_to_all | solution.py:133
  16.3 0.0 copy-done
  16.3 0.6 %shard_map.38 = bf16[64,8,128]{2,1,0:T(8,128)(2,1)S(1)} custom-call(bf16[2,4]{1,0:T(2,128)(2,1)S(1)} %copy-done, bf16[16,64,128]{2,1,0:T(8,128)(2,1)S(1)} %all_to_all.10.rows_ref, bf16[2048,512]{1,0:T(8,128)(2,1)S(1)} %get-tuple-element.8.orbitals_ref), custom_call_target="tpu_custom_call" | custom-call | tf_op jit(solution)/shard_map/pallas_call | solution.py:105
  16.9 32.7 %all_to_all.11.terms_ref = bf16[64,8,128]{2,1,0:T(8,128)(2,1)S(1)} all-to-all(bf16[64,8,128]{2,1,0:T(8,128)(2,1)S(1)} %shard_map.38), channel_id=1, replica_groups={{720,736,752,768,784,800,816,832,848,864,880,896,912,928,944,960,976,99..., dimensions={0} | all-to-all | bytes 262144 | tf_op jit(solution)/shard_map/all_to_all | solution.py:133
  49.6 0.7 %shard_map.39 = f32[4,8,32]{2,1,0:T(8,128)} custom-call(bf16[64,8,128]{2,1,0:T(8,128)(2,1)S(1)} %all_to_all.11.terms_ref), custom_call_target="tpu_custom_call" | custom-call | tf_op jit(solution)/shard_map/pallas_call | solution.py:123
Async XLA Ops:
  0.0 16.3 %copy-start = (bf16[2,4]{1,0:T(2,128)(2,1)S(1)}, bf16[2,4]{1,0:T(2,128)(2,1)}, u32[]{:S(2)}) copy-start(bf16[2,4]{1,0:T(2,128)(2,1)} %weights_ref.1) | copy-start | bytes 52

commit v5 on v4

--- a/solution.py
+++ b/solution.py
@@ -84,18 +84,22 @@
         right = orbitals_ref[s * ns : (s + step) * ns, :]
         term = jnp.dot(left, right, preferred_element_type=jnp.float32)
         total = term if total is None else total + term
+    half = orbitals_ref.shape[1] // out_ref.shape[0] // 2
+    sent = total.T.reshape(out_ref.shape[0], 2 * half, height)
+    sent = jnp.concatenate([sent[:, :half], sent[:, half:]], axis=2).astype(out_ref.dtype)
+    weights = weights_ref[...].astype(jnp.float32)
     width = height // lams
-    weights = weights_ref[...].astype(jnp.float32)
-    terms = []
-    for k in range(korb):
-        term = weights[0:1, k : k + 1] * total[:width]
-        for l in range(1, lams):
-            term = term + weights[l : l + 1, k : k + 1] * total[l * width : (l + 1) * width]
-        terms.append(term)
-    sent = jnp.concatenate(terms, axis=0).astype(out_ref.dtype).T
-    sent = sent.reshape(out_ref.shape)
+    lanes = [
+        jnp.concatenate([jnp.broadcast_to(weights[l : l + 1, k : k + 1], (1, width)) for l in range(lams)], axis=1)
+        for k in range(korb)
+    ]
+    spread = jnp.concatenate(
+        [jnp.concatenate(lanes[k : k + 2], axis=1) for k in range(0, korb, 2)], axis=0
+    ).astype(out_ref.dtype)
     for p, owner in enumerate(lam_order(out_ref.shape[0])):
-        out_ref[p] = sent[owner]
+        for g in range(half // 2):
+            out_ref[p, g] = sent[owner, 2 * g : 2 * g + 2]
+        out_ref[p, half // 2] = spread
 
 
 def second(weights, rows, orbitals, owners):
@@ -104,7 +108,7 @@
     orbs = orbitals.shape[1]
     return pl.pallas_call(
         second_kernel,
-        out_shape=pltpu.VMEM((owners, orbs // owners, korb * height // lams), rows.dtype),
+        out_shape=pltpu.VMEM((owners, orbs // owners // 4 + 1, 2, 2 * height), rows.dtype),
         in_specs=[VMEM, VMEM, VMEM],
         out_specs=VMEM,
         compiler_params=PARAMS,
@@ -112,17 +116,36 @@
 
 
 def last_kernel(terms_ref, out_ref):
-    korb, _, width = out_ref.shape
-    total = jnp.sum(terms_ref[...].astype(jnp.float32), axis=0)
-    for k in range(korb):
-        out_ref[k] = total[:, k * width : (k + 1) * width]
+    korb, js, width = out_ref.shape
+    owners, groups, pair, wide = terms_ref.shape
+    lanes = wide // 2
+    rows = [terms_ref[:, g].reshape(owners * pair, wide).astype(jnp.float32) for g in range(groups)]
+    own = rows.pop()
+    even = lax.rem(lax.broadcasted_iota(jnp.int32, own.shape, 0), pair) == 0
+    low = lax.broadcasted_iota(jnp.int32, own.shape, 1) < lanes
+    count = owners * pair
+    for r in range(pair):
+        near = jnp.where(even, own, pltpu.roll(own, 1, 0)) if r == 0 else jnp.where(even, pltpu.roll(own, count - 1, 0), own)
+        far = pltpu.roll(near, lanes, 1)
+        for side in range(2):
+            k = 2 * r + side
+            weight = jnp.where(low, near, far) if side == 0 else jnp.where(low, far, near)
+            for g in range(groups - 1):
+                total = jnp.sum((rows[g] * weight).reshape(count // 8, 8, wide), axis=0)
+                total = total[0:2] + total[2:4] + total[4:6] + total[6:8]
+                for h in range(2):
+                    block = total[:, h * lanes : (h + 1) * lanes]
+                    value = block[:, :width]
+                    for l in range(1, lanes // width):
+                        value = value + block[:, l * width : (l + 1) * width]
+                    row = h * (js // 2) + 2 * g
+                    out_ref[k, row : row + 2] = value
 
 
-def last(terms, korb):
-    _, js, height = terms.shape
+def last(terms, korb, js, width):
     return pl.pallas_call(
         last_kernel,
-        out_shape=jax.ShapeDtypeStruct((korb, js, height // korb), jnp.float32),
+        out_shape=jax.ShapeDtypeStruct((korb, js, width), jnp.float32),
         in_specs=[VMEM],
         out_specs=VMEM,
         compiler_params=PARAMS,
@@ -138,7 +161,8 @@
     rows = exchange(halfway, "nu", nu_order(nu_owners))
     sent = second(lam_orbitals, rows, orbitals, lam_owners)
     terms = exchange(sent, "lam", lam_order(lam_owners))
-    return last(terms, lam_orbitals.shape[1]).transpose(0, 2, 1)
+    orbs = orbitals.shape[1]
+    return last(terms, lam_orbitals.shape[1], orbs // lam_owners, orbs // nu_owners).transpose(0, 2, 1)
 
 
 def solution(mesh):

time: 50.5 us -> 50.3 us (level)
  blocking collectives: 46.6 us -> 45.9 us
    all_to_all x2, blocking collectives: 46.6 us -> 45.9 us  [exchange(): lax.all_to_all(blocks, axis, split_axis=0, concat_axis=0, tiled=True, axi...]
where the time goes in v5:
time: 50.3 us; the launch traced here: 50.1 us
  blocking collectives  45.9 us (91%)
  Pallas kernels  4.14 us (8%)
    all_to_all x2, blocking collectives, exchange(): lax.all_to_all(blocks, axis, split_axis=0, concat_axis=0, tiled=True, axi...  45.9 us
    pallas_call x1, Pallas kernels, first(): pl.pallas_call(first_kernel, out_shape=(pltpu.VMEM((owners, lams * orbs /...  2.41 us
    pallas_call x1, Pallas kernels, last(): pl.pallas_call(last_kernel, out_shape=jax.ShapeDtypeStruct((korb, js, wid...  1.06 us

profile of v5, /device:TPU:1, one launch (start us, length us, event | category | flops | bytes accessed | tf_op | source)
XLA Modules:
  0.0 50.1 jit_solution(10632401927162247910)
XLA Ops:
  0.0 0.0 copy-start
  0.0 2.4 %shard_map.37 = (bf16[16,64,128]{2,1,0:T(8,128)(2,1)S(1)}, bf16[2048,512]{1,0:T(8,128)(2,1)S(1)}) custom-call(bf16[2,2048,128]{2,1,0:T(8,128)(2,1)} %integrals_hbm.1, bf16[2048,512]{1,0:T(8,128)(2,1)} %orbitals_hbm.1), custom_call_target="tpu_custom_call" | custom-call | tf_op jit(solution)/shard_map/pallas_call | solution.py:60
  2.4 13.8 %all_to_all.10.rows_ref = bf16[16,64,128]{2,1,0:T(8,128)(2,1)S(1)} all-to-all(bf16[16,64,128]{2,1,0:T(8,128)(2,1)S(1)} %get-tuple-element.7), channel_id=1, replica_groups={{12,13,14,15,0,1,2,3,4,5,6,7,8,9,10,11},{28,29,30,31,16,17,18,19,20,21,..., dimensions={0} | all-to-all | bytes 524288 | tf_op jit(solution)/shard_map/all_to_all | solution.py:156
  16.3 0.0 copy-done
  16.3 0.7 %shard_map.38 = bf16[64,3,2,128]{3,2,1,0:T(2,128)(2,1)S(1)} custom-call(bf16[2,4]{1,0:T(2,128)(2,1)S(1)} %copy-done, bf16[16,64,128]{2,1,0:T(8,128)(2,1)S(1)} %all_to_all.10.rows_ref, bf16[2048,512]{1,0:T(8,128)(2,1)S(1)} %get-tuple-element.8.orbitals_ref), custom_call_target="tpu_custom_call" | custom-call | tf_op jit(solution)/shard_map/pallas_call | solution.py:109
  17.0 32.1 %all_to_all.11.terms_ref = bf16[64,3,2,128]{3,2,1,0:T(2,128)(2,1)S(1)} all-to-all(bf16[64,3,2,128]{3,2,1,0:T(2,128)(2,1)S(1)} %shard_map.38), channel_id=1, replica_groups={{720,736,752,768,784,800,816,832,848,864,880,896,912,928,944,960,976,99..., dimensions={0} | all-to-all | bytes 196608 | tf_op jit(solution)/shard_map/all_to_all | solution.py:156
  49.0 1.1 %shard_map.39 = f32[4,8,32]{2,1,0:T(8,128)} custom-call(bf16[64,3,2,128]{3,2,1,0:T(2,128)(2,1)S(1)} %all_to_all.11.terms_ref), custom_call_target="tpu_custom_call" | custom-call | tf_op jit(solution)/shard_map/pallas_call | solution.py:146
Async XLA Ops:
  0.0 16.3 %copy-start = (bf16[2,4]{1,0:T(2,128)(2,1)S(1)}, bf16[2,4]{1,0:T(2,128)(2,1)}, u32[]{:S(2)}) copy-start(bf16[2,4]{1,0:T(2,128)(2,1)} %weights_ref.1) | copy-start | bytes 52

commit v6 on v5

--- a/solution.py
+++ b/solution.py
@@ -77,13 +77,8 @@
     lams, korb = weights_ref.shape
     owners, height, ns = rows_ref.shape
     place = {owner: p for p, owner in enumerate(nu_order(owners))}
-    step = 2
-    total = None
-    for s in range(0, owners, step):
-        left = jnp.concatenate([rows_ref[place[s + t]] for t in range(step)], axis=1)
-        right = orbitals_ref[s * ns : (s + step) * ns, :]
-        term = jnp.dot(left, right, preferred_element_type=jnp.float32)
-        total = term if total is None else total + term
+    left = jnp.concatenate([rows_ref[place[owner]] for owner in range(owners)], axis=1)
+    total = jnp.dot(left, orbitals_ref[...], preferred_element_type=jnp.float32)
     half = orbitals_ref.shape[1] // out_ref.shape[0] // 2
     sent = total.T.reshape(out_ref.shape[0], 2 * half, height)
     sent = jnp.concatenate([sent[:, :half], sent[:, half:]], axis=2).astype(out_ref.dtype)

time: 50.3 us -> 50.3 us (level)
  no operation moved by 1% of the time
where the time goes in v6:
time: 50.3 us; the launch traced here: 50.1 us
  blocking collectives  45.9 us (91%)
  Pallas kernels  4.14 us (8%)
    all_to_all x2, blocking collectives, exchange(): lax.all_to_all(blocks, axis, split_axis=0, concat_axis=0, tiled=True, axi...  45.9 us
    pallas_call x1, Pallas kernels, first(): pl.pallas_call(first_kernel, out_shape=(pltpu.VMEM((owners, lams * orbs /...  2.41 us
    pallas_call x1, Pallas kernels, last(): pl.pallas_call(last_kernel, out_shape=jax.ShapeDtypeStruct((korb, js, wid...  1.06 us

profile of v6, /device:TPU:1, one launch (start us, length us, event | category | flops | bytes accessed | tf_op | source)
XLA Modules:
  0.0 50.1 jit_solution(3132679461610239973)
XLA Ops:
  0.0 0.0 copy-start
  0.0 2.4 %shard_map.37 = (bf16[16,64,128]{2,1,0:T(8,128)(2,1)S(1)}, bf16[2048,512]{1,0:T(8,128)(2,1)S(1)}) custom-call(bf16[2,2048,128]{2,1,0:T(8,128)(2,1)} %integrals_hbm.1, bf16[2048,512]{1,0:T(8,128)(2,1)} %orbitals_hbm.1), custom_call_target="tpu_custom_call" | custom-call | tf_op jit(solution)/shard_map/pallas_call | solution.py:60
  2.4 13.8 %all_to_all.10.rows_ref = bf16[16,64,128]{2,1,0:T(8,128)(2,1)S(1)} all-to-all(bf16[16,64,128]{2,1,0:T(8,128)(2,1)S(1)} %get-tuple-element.7), channel_id=1, replica_groups={{12,13,14,15,0,1,2,3,4,5,6,7,8,9,10,11},{28,29,30,31,16,17,18,19,20,21,..., dimensions={0} | all-to-all | bytes 524288 | tf_op jit(solution)/shard_map/all_to_all | solution.py:151
  16.3 0.0 copy-done
  16.3 0.7 %shard_map.38 = bf16[64,3,2,128]{3,2,1,0:T(2,128)(2,1)S(1)} custom-call(bf16[2,4]{1,0:T(2,128)(2,1)S(1)} %copy-done, bf16[16,64,128]{2,1,0:T(8,128)(2,1)S(1)} %all_to_all.10.rows_ref, bf16[2048,512]{1,0:T(8,128)(2,1)S(1)} %get-tuple-element.8.orbitals_ref), custom_call_target="tpu_custom_call" | custom-call | tf_op jit(solution)/shard_map/pallas_call | solution.py:104
  17.0 32.1 %all_to_all.11.terms_ref = bf16[64,3,2,128]{3,2,1,0:T(2,128)(2,1)S(1)} all-to-all(bf16[64,3,2,128]{3,2,1,0:T(2,128)(2,1)S(1)} %shard_map.38), channel_id=1, replica_groups={{720,736,752,768,784,800,816,832,848,864,880,896,912,928,944,960,976,99..., dimensions={0} | all-to-all | bytes 196608 | tf_op jit(solution)/shard_map/all_to_all | solution.py:151
  49.0 1.1 %shard_map.39 = f32[4,8,32]{2,1,0:T(8,128)} custom-call(bf16[64,3,2,128]{3,2,1,0:T(2,128)(2,1)S(1)} %all_to_all.11.terms_ref), custom_call_target="tpu_custom_call" | custom-call | tf_op jit(solution)/shard_map/pallas_call | solution.py:141
Async XLA Ops:
  0.0 16.3 %copy-start = (bf16[2,4]{1,0:T(2,128)(2,1)S(1)}, bf16[2,4]{1,0:T(2,128)(2,1)}, u32[]{:S(2)}) copy-start(bf16[2,4]{1,0:T(2,128)(2,1)} %weights_ref.1) | copy-start | bytes 52

commit v7 on v6

--- a/solution.py
+++ b/solution.py
@@ -19,7 +19,7 @@
 
 
 def lam_order(size):
-    return [(45 + p) % size for p in range(size)]
+    return [(61 + p) % size for p in range(size)]
 
 
 def first_kernel(integrals_hbm, orbitals_hbm, out_ref, orbitals, integrals, sems):

time: 50.3 us -> 50.3 us (level)
  no operation moved by 1% of the time
where the time goes in v7:
time: 50.3 us; the launch traced here: 50.1 us
  blocking collectives  46 us (91%)
  Pallas kernels  4.14 us (8%)
    all_to_all x2, blocking collectives, exchange(): lax.all_to_all(blocks, axis, split_axis=0, concat_axis=0, tiled=True, axi...  46 us
    pallas_call x1, Pallas kernels, first(): pl.pallas_call(first_kernel, out_shape=(pltpu.VMEM((owners, lams * orbs /...  2.41 us
    pallas_call x1, Pallas kernels, last(): pl.pallas_call(last_kernel, out_shape=jax.ShapeDtypeStruct((korb, js, wid...  1.06 us

profile of v7, /device:TPU:1, one launch (start us, length us, event | category | flops | bytes accessed | tf_op | source)
XLA Modules:
  0.0 50.1 jit_solution(5248136201724892473)
XLA Ops:
  0.0 0.0 copy-start
  0.0 2.4 %shard_map.37 = (bf16[16,64,128]{2,1,0:T(8,128)(2,1)S(1)}, bf16[2048,512]{1,0:T(8,128)(2,1)S(1)}) custom-call(bf16[2,2048,128]{2,1,0:T(8,128)(2,1)} %integrals_hbm.1, bf16[2048,512]{1,0:T(8,128)(2,1)} %orbitals_hbm.1), custom_call_target="tpu_custom_call" | custom-call | tf_op jit(solution)/shard_map/pallas_call | solution.py:60
  2.4 13.8 %all_to_all.10.rows_ref = bf16[16,64,128]{2,1,0:T(8,128)(2,1)S(1)} all-to-all(bf16[16,64,128]{2,1,0:T(8,128)(2,1)S(1)} %get-tuple-element.7), channel_id=1, replica_groups={{12,13,14,15,0,1,2,3,4,5,6,7,8,9,10,11},{28,29,30,31,16,17,18,19,20,21,..., dimensions={0} | all-to-all | bytes 524288 | tf_op jit(solution)/shard_map/all_to_all | solution.py:151
  16.3 0.0 copy-done
  16.3 0.7 %shard_map.38 = bf16[64,3,2,128]{3,2,1,0:T(2,128)(2,1)S(1)} custom-call(bf16[2,4]{1,0:T(2,128)(2,1)S(1)} %copy-done, bf16[16,64,128]{2,1,0:T(8,128)(2,1)S(1)} %all_to_all.10.rows_ref, bf16[2048,512]{1,0:T(8,128)(2,1)S(1)} %get-tuple-element.8.orbitals_ref), custom_call_target="tpu_custom_call" | custom-call | tf_op jit(solution)/shard_map/pallas_call | solution.py:104
  17.0 32.1 %all_to_all.11.terms_ref = bf16[64,3,2,128]{3,2,1,0:T(2,128)(2,1)S(1)} all-to-all(bf16[64,3,2,128]{3,2,1,0:T(2,128)(2,1)S(1)} %shard_map.38), channel_id=1, replica_groups={{976,992,1008,0,16,32,48,64,80,96,112,128,144,160,176,192,208,224,240,2..., dimensions={0} | all-to-all | bytes 196608 | tf_op jit(solution)/shard_map/all_to_all | solution.py:151
  49.1 1.1 %shard_map.39 = f32[4,8,32]{2,1,0:T(8,128)} custom-call(bf16[64,3,2,128]{3,2,1,0:T(2,128)(2,1)S(1)} %all_to_all.11.terms_ref), custom_call_target="tpu_custom_call" | custom-call | tf_op jit(solution)/shard_map/pallas_call | solution.py:141
Async XLA Ops:
  0.0 16.3 %copy-start = (bf16[2,4]{1,0:T(2,128)(2,1)S(1)}, bf16[2,4]{1,0:T(2,128)(2,1)}, u32[]{:S(2)}) copy-start(bf16[2,4]{1,0:T(2,128)(2,1)} %weights_ref.1) | copy-start | bytes 52

commit v8 on v6

--- a/solution.py
+++ b/solution.py
@@ -15,7 +15,7 @@
 
 
 def nu_order(size):
-    return [(12 + p) % size for p in range(size)]
+    return [(12 - p) % size for p in range(size)]
 
 
 def lam_order(size):

time: 50.3 us -> 50.3 us (level)
  no operation moved by 1% of the time
where the time goes in v8:
time: 50.3 us; the launch traced here: 50.2 us
  blocking collectives  46 us (91%)
  Pallas kernels  4.14 us (8%)
    all_to_all x2, blocking collectives, exchange(): lax.all_to_all(blocks, axis, split_axis=0, concat_axis=0, tiled=True, axi...  46 us
    pallas_call x1, Pallas kernels, first(): pl.pallas_call(first_kernel, out_shape=(pltpu.VMEM((owners, lams * orbs /...  2.41 us
    pallas_call x1, Pallas kernels, last(): pl.pallas_call(last_kernel, out_shape=jax.ShapeDtypeStruct((korb, js, wid...  1.06 us

profile of v8, /device:TPU:1, one launch (start us, length us, event | category | flops | bytes accessed | tf_op | source)
XLA Modules:
  0.0 50.2 jit_solution(12354847046747575806)
XLA Ops:
  0.0 0.0 copy-start
  0.0 2.4 %shard_map.37 = (bf16[16,64,128]{2,1,0:T(8,128)(2,1)S(1)}, bf16[2048,512]{1,0:T(8,128)(2,1)S(1)}) custom-call(bf16[2,2048,128]{2,1,0:T(8,128)(2,1)} %integrals_hbm.1, bf16[2048,512]{1,0:T(8,128)(2,1)} %orbitals_hbm.1), custom_call_target="tpu_custom_call" | custom-call | tf_op jit(solution)/shard_map/pallas_call | solution.py:60
  2.4 13.9 %all_to_all.10.rows_ref = bf16[16,64,128]{2,1,0:T(8,128)(2,1)S(1)} all-to-all(bf16[16,64,128]{2,1,0:T(8,128)(2,1)S(1)} %get-tuple-element.7), channel_id=1, replica_groups={{12,11,10,9,8,7,6,5,4,3,2,1,0,15,14,13},{28,27,26,25,24,23,22,21,20,19,..., dimensions={0} | all-to-all | bytes 524288 | tf_op jit(solution)/shard_map/all_to_all | solution.py:151
  16.3 0.0 copy-done
  16.3 0.7 %shard_map.38 = bf16[64,3,2,128]{3,2,1,0:T(2,128)(2,1)S(1)} custom-call(bf16[2,4]{1,0:T(2,128)(2,1)S(1)} %copy-done, bf16[16,64,128]{2,1,0:T(8,128)(2,1)S(1)} %all_to_all.10.rows_ref, bf16[2048,512]{1,0:T(8,128)(2,1)S(1)} %get-tuple-element.8.orbitals_ref), custom_call_target="tpu_custom_call" | custom-call | tf_op jit(solution)/shard_map/pallas_call | solution.py:104
  17.0 32.1 %all_to_all.11.terms_ref = bf16[64,3,2,128]{3,2,1,0:T(2,128)(2,1)S(1)} all-to-all(bf16[64,3,2,128]{3,2,1,0:T(2,128)(2,1)S(1)} %shard_map.38), channel_id=1, replica_groups={{720,736,752,768,784,800,816,832,848,864,880,896,912,928,944,960,976,99..., dimensions={0} | all-to-all | bytes 196608 | tf_op jit(solution)/shard_map/all_to_all | solution.py:151
  49.1 1.1 %shard_map.39 = f32[4,8,32]{2,1,0:T(8,128)} custom-call(bf16[64,3,2,128]{3,2,1,0:T(2,128)(2,1)S(1)} %all_to_all.11.terms_ref), custom_call_target="tpu_custom_call" | custom-call | tf_op jit(solution)/shard_map/pallas_call | solution.py:141
Async XLA Ops:
  0.0 16.3 %copy-start = (bf16[2,4]{1,0:T(2,128)(2,1)S(1)}, bf16[2,4]{1,0:T(2,128)(2,1)}, u32[]{:S(2)}) copy-start(bf16[2,4]{1,0:T(2,128)(2,1)} %weights_ref.1) | copy-start | bytes 52
